TPU v7x, 32 devices: a whole 2x2x4 slice. The times are simulated.
32 devices in a mesh: passage: 2 (over x), brick: 16 (over z, y, core).
Axes of the slice: x: 2, y: 2, z: 4, core: 2. Of those that a mesh axis runs over, the one named last changes fastest.
Arguments:
- jac_blocks: bfloat16 [2, 25, 16, 8192], P('passage', None, None, 'brick'), may hold values from -6 to 6
- psi_start: float32 [2, 10, 16, 64, 128], P('passage', None, 'brick'), may hold values from -6 to 6
- source: float32 [2, 10, 16, 64, 128], P('passage', None, 'brick'), may hold values from -6 to 6
- pseudo_step: float32 [2, 16, 64, 128], P('passage', 'brick'), may hold values from 0.1 to 0.4
- dissipation: float32 [2, 16, 64, 128], P('passage', 'brick'), may hold values from 0.04 to 0.15
- freq_volume: float32 [2, 16, 64, 128], P('passage', 'brick'), may hold values from 0.2 to 2
- normals: float32 [2, 3, 16, 64], P('passage', None, 'brick'), may hold values from -6 to 6
- face_owner: int32 [2, 1024, 1], P('passage', 'brick'), may hold values from 0 to 15; in each aligned block of 64 rows (0 to 63, 64 to 127, ..., all dimensions but the last counted through in order) at most 16 rows name the same one
- face_slot: int32 [2, 1024], P('passage', 'brick'), may hold values from 0 to 255
Outputs:
- adjoint: float32 [2, 10, 16, 64, 128], P('passage', None, 'brick')
- sensitivity: float32 [2, 6, 4096], P('passage', None, 'brick')
Inputs may be any that keep to these rules, and one draw needn't show every extreme that they name: `face_owner`: in the 64 faces of one device (aligned blocks of the rows), no brick is named by more than 16 faces, and in some block some brick is named by exactly 16.
All inputs are finite; a program needn't handle non-finite values.
Results may differ from a plain program's by a relative error of at most 0.0003.
Values may be sent and summed in bfloat16 or wider, within the bound.
A program may use at most 64 MiB of HBM per device.

v0:
```python
import math
import jax
import jax.numpy as jnp
from jax import lax
from jax.sharding import PartitionSpec as P

NODE_DEV = 256
SWEEPS = 2
ND = 1
BLADES = 36


def padded(value, sides, width, wrap):
    for axis, dim in sides:
        peers, length = (lax.axis_size(axis), value.shape[dim])
        up = [(i, (i + 1) % peers) for i in range(peers if wrap else peers - 1)]
        down = [(j, i) for i, j in up]
        last = lax.slice_in_dim(value, length - width, length, axis=dim)
        initial = lax.slice_in_dim(value, 0, width, axis=dim)
        before = lax.ppermute(last, axis, up)
        after = lax.ppermute(initial, axis, down)
        value = jnp.concatenate([before, value, after], axis=dim)
    return value


def rotate(rim, turn):
    cosine = math.cos(turn)
    sine = math.sin(turn)
    real_part = rim[:, :5]
    imag_part = rim[:, 5:]
    return jnp.concatenate(
        [real_part * cosine - imag_part * sine, real_part * sine + imag_part * cosine], axis=1
    )


def transpose_apply(tiles, diff):
    total_real = jnp.zeros_like(diff[:, :5])
    total_imag = jnp.zeros_like(diff[:, :5])
    for row_index in range(5):
        column = tiles[:, row_index * 5 : row_index * 5 + 5].astype(jnp.float32)
        total_real = total_real + column * diff[:, row_index : row_index + 1]
        total_imag = total_imag + column * diff[:, 5 + row_index : 6 + row_index]
    return jnp.concatenate([total_real, total_imag], axis=1)


def advance(
    state,
    source,
    pseudo_step,
    dissipation,
    freq_volume,
    convect_fn,
    cycle_index,
    passes,
    phase_angle,
):
    padded_i = padded(state, (("brick", 2),), 1, False)
    padded_j = padded(state.astype(jnp.bfloat16), (("passage", 3),), 1, True).astype(state.dtype)
    below_rim = padded_j[:, :, :, :1]
    above_rim = padded_j[:, :, :, -1:]
    below_rim = jnp.where(cycle_index == 0, rotate(below_rim, -phase_angle), below_rim)
    above_rim = jnp.where(cycle_index == passes - 1, rotate(above_rim, phase_angle), above_rim)
    fixed_j = jnp.concatenate([below_rim, state, above_rim], axis=3)
    padded_k = jnp.pad(state, ((0, 0), (0, 0), (0, 0), (0, 0), (1, 1)))
    beside = padded_i[:, :, 2:] + padded_i[:, :, :-2]
    beside = beside + fixed_j[:, :, :, 2:] + fixed_j[:, :, :, :-2]
    beside = beside + padded_k[..., 2:] + padded_k[..., :-2]
    diff = 0.5 * (padded_i[:, :, 2:] - padded_i[:, :, :-2])
    convect = convect_fn(diff)
    omega = freq_volume[:, None]
    spin = jnp.concatenate([omega * state[:, 5:], -omega * state[:, :5]], axis=1)
    resid = convect + spin + dissipation[:, None] * (6.0 * state - beside) - source
    return state - pseudo_step[:, None] * resid


def body(
    jac_blocks,
    psi_start,
    source,
    pseudo_step,
    dissipation,
    freq_volume,
    normals,
    face_owner,
    face_slot,
):
    passes = lax.axis_size("passage")
    cycle_index = lax.axis_index("passage")
    bricks = lax.axis_size("brick")
    planes = psi_start.shape[2]
    width_j = psi_start.shape[3]
    width_k = psi_start.shape[4]
    phase_angle = 2.0 * math.pi * ND * passes / BLADES
    relaid = lax.all_to_all(jac_blocks, "brick", split_axis=2, concat_axis=3, tiled=True)
    tiles = relaid.reshape(1, 25, planes, width_j, width_k)

    def convect_fn(diff):
        return transpose_apply(tiles, diff)

    state = psi_start
    for sweep in range(SWEEPS):
        state = advance(
            state,
            source,
            pseudo_step,
            dissipation,
            freq_volume,
            convect_fn,
            cycle_index,
            passes,
            phase_angle,
        )
    wall_state = state[0, :, :, :, 0]
    face_normals = normals[0]
    values = jnp.concatenate(
        [face_normals * wall_state[1:4], face_normals * wall_state[6:9]], axis=0
    )
    values = values.reshape(6, planes * width_j)
    owners = face_owner[0, :, 0]
    slots = face_slot[0]
    node_ids = owners * NODE_DEV + slots
    local_terms = jnp.zeros((6, NODE_DEV * bricks), jnp.float32).at[:, node_ids].add(values)
    summed = lax.psum_scatter(local_terms, "brick", scatter_dimension=1, tiled=True)
    sensitivity = summed[None]
    return (state, sensitivity)


def solution(mesh):
    placed = (
        P("passage", None, None, "brick"),
        P("passage", None, "brick", None, None),
        P("passage", None, "brick", None, None),
        P("passage", "brick", None, None),
        P("passage", "brick", None, None),
        P("passage", "brick", None, None),
        P("passage", None, "brick", None),
        P("passage", "brick", None),
        P("passage", "brick"),
    )
    return jax.shard_map(
        body,
        mesh=mesh,
        in_specs=placed,
        out_specs=(P("passage", None, "brick", None, None), P("passage", None, "brick")),
        check_vma=False,
    )
```

profile of v0, /device:TPU:0, one launch (start us, length us, event | category | flops | bytes accessed | tf_op | source)
XLA Modules:
  0.0 128.0 jit_solution(5724360956886795302)
XLA Ops:
  7.2 2.5 %collective-permute-start.1 = (f32[1,10,1,64,128]{4,3,1,2,0:T(8,128)}, f32[1,10,1,64,128]{4,3,1,2,0:T(8,128)S(1)}, u32[]{:S(2)}, u32[]{:S(2)}) collective-permute-start(f32[1,10,1,64,128]{4,3,1,2,0:T(8,128)} %bitcast.71), channel_id=1, source_target_pairs={{0,1},{1,2},{2,3},{3,4},{4,5},{5,6},{6,7},{7,8},{8,9},{9,10},{10,1... | collective-permute-start | bytes 983048 | tf_op jit(solution)/shard_map/ppermute | solution.py:20
  9.8 1.3 %collective-permute-start = (f32[1,10,1,64,128]{4,3,1,2,0:T(8,128)}, f32[1,10,1,64,128]{4,3,1,2,0:T(8,128)S(1)}, u32[]{:S(2)}, u32[]{:S(2)}) collective-permute-start(f32[1,10,1,64,128]{4,3,1,2,0:T(8,128)} %bitcast.72), channel_id=1, source_target_pairs={{1,0},{2,1},{3,2},{4,3},{5,4},{6,5},{7,6},{8,7},{9,8},{10,9},{11,1... | collective-permute-start | bytes 983048 | tf_op jit(solution)/shard_map/ppermute | solution.py:21
  11.1 1.0 bitcast_convert_fusion
  12.1 2.4 %collective-permute-start.2 = (bf16[1,10,1,1,128]{4,3,1,2,0:T(2,128)(2,1)S(1)}, bf16[1,10,1,1,128]{4,3,1,2,0:T(2,128)(2,1)S(1)}, u32[]{:S(2)}, u32[]{:S(2)}) collective-permute-start(bf16[1,10,1,1,128]{4,3,1,2,0:T(2,128)(2,1)S(1)} %get-tuple-element.64), channel_id=1, source_target_pairs={{0,16},{16,0},{1,17},{17,1},{2,18},{18,2},{3,19},{19,3},{4,20},{20... | collective-permute-start | bytes 7688 | tf_op jit(solution)/shard_map/ppermute | solution.py:20
  14.5 0.1 collective-permute-start.3
  14.5 2.0 %copy.66 = bf16[1,25,16,512]{3,1,0,2:T(8,128)(2,1)} copy(bf16[1,25,16,512]{3,2,1,0:T(8,128)(2,1)} %param.9) | data formatting | bytes 819200 | tf_op args[0]
  16.6 8.9 %all-to-all-start = ((bf16[1,25,16,512]{3,1,0,2:T(8,128)(2,1)}), bf16[1,25,16,512]{3,1,0,2:T(8,128)(2,1)S(1)}, u32[]{:S(2)}, u32[]{:S(2)}) async-start(bf16[1,25,16,512]{3,1,0,2:T(8,128)(2,1)} %copy.66), calls=%async_computation | async-start | bytes 1048576 | tf_op jit(solution)/shard_map/all_to_all | solution.py:94
  25.5 0.0 reduce-scatter.2.cloned.1.call-start
  25.9 0.0 copy-start.5
  25.9 13.9 %all-to-all-done = bf16[1,25,16,512]{3,1,0,2:T(8,128)(2,1)S(1)} async-done(((bf16[1,25,16,512]{3,1,0,2:T(8,128)(2,1)}), bf16[1,25,16,512]{3,1,0,2:T(8,128)(2,1)S(1)}, u32[]{:S(2)}, u32[]{:S(2)}) %all-to-all-start) | async-done | bytes 409632 | tf_op jit(solution)/shard_map/all_to_all | solution.py:94
  39.8 0.2 copy.67
  40.0 0.2 reshape.329
  40.3 0.1 fusion.29
  40.4 0.1 fusion.25
  40.5 0.3 fusion.50
  40.8 1.6 %collective-permute-start.6 = (bf16[1,10,1,1,128]{4,3,1,2,0:T(2,128)(2,1)S(1)}, bf16[1,10,1,1,128]{4,3,1,2,0:T(2,128)(2,1)S(1)}, u32[]{:S(2)}, u32[]{:S(2)}) collective-permute-start(bf16[1,10,1,1,128]{4,3,1,2,0:T(2,128)(2,1)S(1)} %get-tuple-element.62), channel_id=1, source_target_pairs={{0,16},{16,0},{1,17},{17,1},{2,18},{18,2},{3,19},{19,3},{4,20},{20... | collective-permute-start | bytes 7688 | tf_op jit(solution)/shard_map/ppermute | solution.py:20
  42.4 0.5 collective-permute-start.7
  42.9 1.5 %collective-permute-start.5 = (f32[1,10,1,64,128]{4,3,1,2,0:T(8,128)S(1)}, f32[1,10,1,64,128]{4,3,1,2,0:T(8,128)S(1)}, u32[]{:S(2)}, u32[]{:S(2)}) collective-permute-start(f32[1,10,1,64,128]{4,3,1,2,0:T(8,128)S(1)} %get-tuple-element.21), channel_id=1, source_target_pairs={{0,1},{1,2},{2,3},{3,4},{4,5},{5,6},{6,7},{7,8},{8,9},{9,10},{10,1... | collective-permute-start | bytes 983048 | tf_op jit(solution)/shard_map/ppermute | solution.py:20
  44.5 1.3 %collective-permute-start.4 = (f32[1,10,1,64,128]{4,3,1,2,0:T(8,128)S(1)}, f32[1,10,1,64,128]{4,3,1,2,0:T(8,128)S(1)}, u32[]{:S(2)}, u32[]{:S(2)}) collective-permute-start(f32[1,10,1,64,128]{4,3,1,2,0:T(8,128)S(1)} %get-tuple-element.21), channel_id=1, source_target_pairs={{1,0},{2,1},{3,2},{4,3},{5,4},{6,5},{7,6},{8,7},{9,8},{10,9},{11,1... | collective-permute-start | bytes 983048 | tf_op jit(solution)/shard_map/ppermute | solution.py:21
  45.8 0.2 collective-permute-done.7
  46.1 2.3 %collective-permute-done.4 = f32[1,10,1,64,128]{4,3,1,2,0:T(8,128)S(1)} collective-permute-done((f32[1,10,1,64,128]{4,3,1,2,0:T(8,128)S(1)}, f32[1,10,1,64,128]{4,3,1,2,0:T(8,128)S(1)}, u32[]{:S(2)}, u32[]{:S(2)}) %collective-permute-start.4) | collective-permute-done | bytes 327712 | tf_op jit(solution)/shard_map/ppermute | solution.py:21
  48.5 0.0 copy-start.6
  48.5 0.1 fusion.33
  48.6 0.1 fusion.37
  48.7 0.4 fusion.17
  49.1 0.0 copy-start.2
  49.1 0.1 slice_reduce_fusion.1
  49.3 0.1 copy.84
  49.4 2.2 %scatter_custom_fusion = f32[6,4096]{0,1:T(8,128)} fusion(s32[64]{0:T(128)S(1)} %fusion.49, f32[]{:T(128)} %constant.11.clone.1, f32[6,1,64]{0,2,1:T(8,128)S(1)} %copy.84), kind=kCustom, calls=%fused_computation.1 | custom fusion | flops 384 | bytes 131076 | tf_op jit(solution)/shard_map/scatter-add | solution.py:122
  51.6 0.0 reduce-scatter.2.cloned.1.call-update
  51.6 68.0 %reduce-scatter.2.cloned.1.call-done = f32[6,256]{0,1:T(8,128)} async-done(((f32[6,4096]{0,1:T(8,128)}), f32[6,256]{0,1:T(8,128)}) %reduce-scatter.2.cloned.1.call-update) | async-done | bytes 6160 | tf_op jit(solution)/shard_map/reduce_scatter | solution.py:123
  119.6 1.6 %copy.82 = f32[1,6,256]{2,0,1:T(1,128)} copy(f32[1,6,256]{1,2,0:T(8,128)} %bitcast.82) | data formatting | bytes 12288
  (40 shorter events, 0.4 us)
Async XLA Ops:
  7.2 18.4 %copy-start = (f32[1,10,1,64,128]{4,3,2,1,0:T(8,128)S(1)}, f32[1,10,1,64,128]{4,3,2,1,0:T(8,128)}, u32[]{:S(2)}) copy-start(f32[1,10,1,64,128]{4,3,2,1,0:T(8,128)} %param.10) | copy-start | bytes 983044
  7.2 18.4 %copy-start.3 = (f32[1,1,64,128]{3,2,1,0:T(8,128)S(1)}, f32[1,1,64,128]{3,2,1,0:T(8,128)}, u32[]{:S(2)}) copy-start(f32[1,1,64,128]{3,2,1,0:T(8,128)} %param.14) | copy-start | bytes 98308
  7.2 18.4 %copy-start.7 = (s32[1,64]{1,0:T(1,128)S(1)}, s32[1,64]{1,0:T(1,128)}, u32[]{:S(2)}) copy-start(s32[1,64]{1,0:T(1,128)} %param.17) | copy-start | bytes 772
  7.2 18.4 %copy-start.8 = (s32[1,64,1]{1,2,0:T(1,128)S(1)}, s32[1,64,1]{1,2,0:T(1,128)}, u32[]{:S(2)}) copy-start(s32[1,64,1]{1,2,0:T(1,128)} %param.16) | copy-start | bytes 772
  7.2 18.6 %collective-permute-start.1 = (f32[1,10,1,64,128]{4,3,1,2,0:T(8,128)}, f32[1,10,1,64,128]{4,3,1,2,0:T(8,128)S(1)}, u32[]{:S(2)}, u32[]{:S(2)}) collective-permute-start(f32[1,10,1,64,128]{4,3,1,2,0:T(8,128)} %bitcast.71), channel_id=1, source_target_pairs={{0,1},{1,2},{2,3},{3,4},{4,5},{5,6},{6,7},{7,8},{8,9},{9,10},{10,1... | collective-permute-start | bytes 983048 | tf_op jit(solution)/shard_map/ppermute | solution.py:20
  9.8 16.0 %collective-permute-start = (f32[1,10,1,64,128]{4,3,1,2,0:T(8,128)}, f32[1,10,1,64,128]{4,3,1,2,0:T(8,128)S(1)}, u32[]{:S(2)}, u32[]{:S(2)}) collective-permute-start(f32[1,10,1,64,128]{4,3,1,2,0:T(8,128)} %bitcast.72), channel_id=1, source_target_pairs={{1,0},{2,1},{3,2},{4,3},{5,4},{6,5},{7,6},{8,7},{9,8},{10,9},{11,1... | collective-permute-start | bytes 983048 | tf_op jit(solution)/shard_map/ppermute | solution.py:21
  12.1 13.6 %collective-permute-start.2 = (bf16[1,10,1,1,128]{4,3,1,2,0:T(2,128)(2,1)S(1)}, bf16[1,10,1,1,128]{4,3,1,2,0:T(2,128)(2,1)S(1)}, u32[]{:S(2)}, u32[]{:S(2)}) collective-permute-start(bf16[1,10,1,1,128]{4,3,1,2,0:T(2,128)(2,1)S(1)} %get-tuple-element.64), channel_id=1, source_target_pairs={{0,16},{16,0},{1,17},{17,1},{2,18},{18,2},{3,19},{19,3},{4,20},{20... | collective-permute-start | bytes 7688 | tf_op jit(solution)/shard_map/ppermute | solution.py:20
  14.5 11.2 %collective-permute-start.3 = (bf16[1,10,1,1,128]{4,3,1,2,0:T(2,128)(2,1)S(1)}, bf16[1,10,1,1,128]{4,3,1,2,0:T(2,128)(2,1)S(1)}, u32[]{:S(2)}, u32[]{:S(2)}) collective-permute-start(bf16[1,10,1,1,128]{4,3,1,2,0:T(2,128)(2,1)S(1)} %get-tuple-element.65), channel_id=1, source_target_pairs={{16,0},{0,16},{17,1},{1,17},{18,2},{2,18},{19,3},{3,19},{20,4},{4,... | collective-permute-start | bytes 7688 | tf_op jit(solution)/shard_map/ppermute | solution.py:21
  16.6 23.2 %all-to-all-start = ((bf16[1,25,16,512]{3,1,0,2:T(8,128)(2,1)}), bf16[1,25,16,512]{3,1,0,2:T(8,128)(2,1)S(1)}, u32[]{:S(2)}, u32[]{:S(2)}) async-start(bf16[1,25,16,512]{3,1,0,2:T(8,128)(2,1)} %copy.66), calls=%async_computation | async-start | bytes 1048576 | tf_op jit(solution)/shard_map/all_to_all | solution.py:94
  25.5 94.1 %reduce-scatter.2.cloned.1.call-start = ((), (), s32[]{:S(2)}) async-start(), calls=%async_computation.2 | async-start | bytes 2228224 | tf_op jit(solution)/shard_map/reduce_scatter | solution.py:123
  25.8 14.6 %copy-start.1 = (f32[1,10,1,64,128]{4,3,2,1,0:T(8,128)S(1)}, f32[1,10,1,64,128]{4,3,2,1,0:T(8,128)}, u32[]{:S(2)}) copy-start(f32[1,10,1,64,128]{4,3,2,1,0:T(8,128)} %param.11) | copy-start | bytes 983044
  25.8 14.6 %copy-start.4 = (f32[1,1,64,128]{3,2,1,0:T(8,128)S(1)}, f32[1,1,64,128]{3,2,1,0:T(8,128)}, u32[]{:S(2)}) copy-start(f32[1,1,64,128]{3,2,1,0:T(8,128)} %param.13) | copy-start | bytes 98308
  25.9 14.6 %copy-start.5 = (f32[1,1,64,128]{3,2,1,0:T(8,128)S(1)}, f32[1,1,64,128]{3,2,1,0:T(8,128)}, u32[]{:S(2)}) copy-start(f32[1,1,64,128]{3,2,1,0:T(8,128)} %param.12) | copy-start | bytes 98308
  40.8 4.9 %collective-permute-start.6 = (bf16[1,10,1,1,128]{4,3,1,2,0:T(2,128)(2,1)S(1)}, bf16[1,10,1,1,128]{4,3,1,2,0:T(2,128)(2,1)S(1)}, u32[]{:S(2)}, u32[]{:S(2)}) collective-permute-start(bf16[1,10,1,1,128]{4,3,1,2,0:T(2,128)(2,1)S(1)} %get-tuple-element.62), channel_id=1, source_target_pairs={{0,16},{16,0},{1,17},{17,1},{2,18},{18,2},{3,19},{19,3},{4,20},{20... | collective-permute-start | bytes 7688 | tf_op jit(solution)/shard_map/ppermute | solution.py:20
  42.4 3.6 %collective-permute-start.7 = (bf16[1,10,1,1,128]{4,3,1,2,0:T(2,128)(2,1)S(1)}, bf16[1,10,1,1,128]{4,3,1,2,0:T(2,128)(2,1)S(1)}, u32[]{:S(2)}, u32[]{:S(2)}) collective-permute-start(bf16[1,10,1,1,128]{4,3,1,2,0:T(2,128)(2,1)S(1)} %get-tuple-element.63), channel_id=1, source_target_pairs={{16,0},{0,16},{17,1},{1,17},{18,2},{2,18},{19,3},{3,19},{20,4},{4,... | collective-permute-start | bytes 7688 | tf_op jit(solution)/shard_map/ppermute | solution.py:21
  42.9 3.1 %collective-permute-start.5 = (f32[1,10,1,64,128]{4,3,1,2,0:T(8,128)S(1)}, f32[1,10,1,64,128]{4,3,1,2,0:T(8,128)S(1)}, u32[]{:S(2)}, u32[]{:S(2)}) collective-permute-start(f32[1,10,1,64,128]{4,3,1,2,0:T(8,128)S(1)} %get-tuple-element.21), channel_id=1, source_target_pairs={{0,1},{1,2},{2,3},{3,4},{4,5},{5,6},{6,7},{7,8},{8,9},{9,10},{10,1... | collective-permute-start | bytes 983048 | tf_op jit(solution)/shard_map/ppermute | solution.py:20
  44.5 4.0 %collective-permute-start.4 = (f32[1,10,1,64,128]{4,3,1,2,0:T(8,128)S(1)}, f32[1,10,1,64,128]{4,3,1,2,0:T(8,128)S(1)}, u32[]{:S(2)}, u32[]{:S(2)}) collective-permute-start(f32[1,10,1,64,128]{4,3,1,2,0:T(8,128)S(1)} %get-tuple-element.21), channel_id=1, source_target_pairs={{1,0},{2,1},{3,2},{4,3},{5,4},{6,5},{7,6},{8,7},{9,8},{10,9},{11,1... | collective-permute-start | bytes 983048 | tf_op jit(solution)/shard_map/ppermute | solution.py:21
  48.5 0.7 copy-start.6
  49.1 2.5 %copy-start.2 = (f32[1,10,1,64,128]{4,3,1,2,0:T(8,128)}, f32[1,10,1,64,128]{4,3,1,2,0:T(8,128)S(1)}, u32[]{:S(2)}) copy-start(f32[1,10,1,64,128]{4,3,1,2,0:T(8,128)S(1)} %fusion.17) | copy-start | bytes 983044
Sparse Core Ops, SparseCore 0:
  51.7 67.8 reduce-scatter.1
where the time goes:
time: 128 us
  waiting for transfers between devices  84.5 us (66%)
  starting transfers between devices  20.1 us (16%)
  between operations  14.5 us (11%)
  other arithmetic  4.52 us (4%)
  local copies, waits for them, and re-layouts  4.46 us (3%)
    reduce_scatter x1, waiting for transfers between devices, body(): lax.psum_scatter(local_terms, 'brick', scatter_dimension=1, tiled=True)  68 us
    all_to_all x1, waiting for transfers between devices, body(): lax.all_to_all(jac_blocks, 'brick', split_axis=2, concat_axis=3, tiled=True)  13.9 us
    all_to_all x1, starting transfers between devices, body(): lax.all_to_all(jac_blocks, 'brick', split_axis=2, concat_axis=3, tiled=True)  8.92 us
    ppermute x4, starting transfers between devices, padded(): before = lax.ppermute(last, axis, up)  7.99 us
    unnamed x20, local copies, waits for them, and re-layouts  3.67 us
    ppermute x4, starting transfers between devices, padded(): after = lax.ppermute(initial, axis, down)  3.2 us
    ppermute x4, waiting for transfers between devices, padded(): after = lax.ppermute(initial, axis, down)  2.58 us
  transfers between devices with their start and end apart: 10, of which 4 were waited for; matrix products, arithmetic and copies ran while one was open for 3% of the time, Pallas kernels for 0%

commit v1 on v0

--- a/solution.py
+++ b/solution.py
@@ -91,7 +91,19 @@
     width_j = psi_start.shape[3]
     width_k = psi_start.shape[4]
     phase_angle = 2.0 * math.pi * ND * passes / BLADES
-    relaid = lax.all_to_all(jac_blocks, "brick", split_axis=2, concat_axis=3, tiled=True)
+    ways, here = (lax.axis_size("brick"), lax.axis_index("brick"))
+    width_2 = jac_blocks.shape[2] // ways
+    lengths = list(jac_blocks.shape)
+    lengths[2] = width_2
+    height = lengths[3]
+    lengths[3] = height * ways
+    full = jnp.zeros(lengths, jac_blocks.dtype)
+    for mask in range(ways):
+        part = lax.dynamic_slice_in_dim(jac_blocks, (here ^ mask) * width_2, width_2, axis=2)
+        if mask:
+            part = lax.ppermute(part, "brick", [(d, d ^ mask) for d in range(ways)])
+        full = lax.dynamic_update_slice_in_dim(full, part, (here ^ mask) * height, axis=3)
+    relaid = full
     tiles = relaid.reshape(1, 25, planes, width_j, width_k)
 
     def convect_fn(diff):

time: 128 us -> 141 us (1.10)
  starting transfers between devices: 20.1 us -> 41.7 us
  waiting for transfers between devices: 84.5 us -> 73.1 us
  local copies, waits for them, and re-layouts: 4.46 us -> 7 us
    ppermute x0 -> x15, starting transfers between devices: none -> 28.7 us  [body(): part = lax.ppermute(part, 'brick', [(d, d ^ mask) for d in range(ways)])]
    all_to_all x1 -> x0, waiting for transfers between devices: 13.9 us -> none  [body(): lax.all_to_all(jac_blocks, 'brick', split_axis=2, concat_axis=3, tiled=True)]
    all_to_all x1 -> x0, starting transfers between devices: 8.92 us -> none  [body(): lax.all_to_all(jac_blocks, 'brick', split_axis=2, concat_axis=3, tiled=True)]
    ppermute x0 -> x15, waiting for transfers between devices: none -> 6.91 us  [body(): part = lax.ppermute(part, 'brick', [(d, d ^ mask) for d in range(ways)])]
    reduce_scatter x1, waiting for transfers between devices: 68 us -> 61.9 us  [body(): lax.psum_scatter(local_terms, 'brick', scatter_dimension=1, tiled=True)]
    dynamic_slice x0 -> x1, local copies, waits for them, and re-layouts: none -> 4.14 us  [body(): lax.dynamic_slice_in_dim(jac_blocks, (here ^ mask) * width_2, width_2, ax...]
    ppermute x4, waiting for transfers between devices: 0.01 us -> 2.91 us  [padded(): before = lax.ppermute(last, axis, up)]
  transfers between devices with their start and end apart: 10 -> 24, of which waited for: 4 -> 10; matrix products, arithmetic and copies ran while one was open for 3% -> 4% of each run, Pallas kernels for 0% -> 0%
where the time goes in v1:
time: 141 us
  waiting for transfers between devices  73.1 us (52%)
  starting transfers between devices  41.7 us (30%)
  between operations  14.8 us (10%)
  local copies, waits for them, and re-layouts  7 us (5%)
  other arithmetic  4.54 us (3%)
    reduce_scatter x1, waiting for transfers between devices, body(): lax.psum_scatter(local_terms, 'brick', scatter_dimension=1, tiled=True)  61.9 us
    ppermute x15, starting transfers between devices, body(): part = lax.ppermute(part, 'brick', [(d, d ^ mask) for d in range(ways)])  28.7 us
    ppermute x4, starting transfers between devices, padded(): before = lax.ppermute(last, axis, up)  9.17 us
    ppermute x15, waiting for transfers between devices, body(): part = lax.ppermute(part, 'brick', [(d, d ^ mask) for d in range(ways)])  6.91 us
    dynamic_slice x1, local copies, waits for them, and re-layouts, body(): lax.dynamic_slice_in_dim(jac_blocks, (here ^ mask) * width_2, width_2, ax...  4.14 us
    ppermute x4, starting transfers between devices, padded(): after = lax.ppermute(initial, axis, down)  3.83 us
    ppermute x4, waiting for transfers between devices, padded(): before = lax.ppermute(last, axis, up)  2.91 us
  transfers between devices with their start and end apart: 24, of which 10 were waited for; matrix products, arithmetic and copies ran while one was open for 4% of the time, Pallas kernels for 0%

profile of v1, /device:TPU:0, one launch (start us, length us, event | category | flops | bytes accessed | tf_op | source)
XLA Modules:
  0.0 141.2 jit_solution(16507652592194224478)
XLA Ops:
  7.3 1.4 %collective-permute-start.15 = (f32[1,10,1,64,128]{4,3,1,2,0:T(8,128)}, f32[1,10,1,64,128]{4,3,1,2,0:T(8,128)S(1)}, u32[]{:S(2)}, u32[]{:S(2)}) collective-permute-start(f32[1,10,1,64,128]{4,3,1,2,0:T(8,128)} %bitcast.77), channel_id=1, source_target_pairs={{1,0},{2,1},{3,2},{4,3},{5,4},{6,5},{7,6},{8,7},{9,8},{10,9},{11,1... | collective-permute-start | bytes 983048 | tf_op jit(solution)/shard_map/ppermute | solution.py:21
  8.7 3.1 %collective-permute-start.16 = (f32[1,10,1,64,128]{4,3,1,2,0:T(8,128)}, f32[1,10,1,64,128]{4,3,1,2,0:T(8,128)S(1)}, u32[]{:S(2)}, u32[]{:S(2)}) collective-permute-start(f32[1,10,1,64,128]{4,3,1,2,0:T(8,128)} %bitcast.78), channel_id=1, source_target_pairs={{0,1},{1,2},{2,3},{3,4},{4,5},{5,6},{6,7},{7,8},{8,9},{9,10},{10,1... | collective-permute-start | bytes 983048 | tf_op jit(solution)/shard_map/ppermute | solution.py:20
  11.9 4.1 %constant_dynamic-slice_fusion = (bf16[1,25,1,512]{3,2,1,0:T(2,128)(2,1)S(1)}, bf16[1,25,1,512]{3,2,1,0:T(2,128)(2,1)S(1)}, bf16[1,25,1,512]{3,2,1,0:T(2,128)(2,...) fusion(bf16[1,25,16,512]{3,2,1,0:T(8,128)(2,1)} %param.9, ...), kind=kLoop, calls=%fused_computation.119 | loop fusion | bytes 819264 | tf_op jit(solution)/shard_map/dynamic_slice | solution.py:102
  16.0 2.7 %collective-permute-start = (bf16[1,25,1,512]{3,2,1,0:T(2,128)(2,1)S(1)}, bf16[1,25,1,512]{3,2,1,0:T(2,128)(2,1)S(1)}, u32[]{:S(2)}, u32[]{:S(2)}) collective-permute-start(bf16[1,25,1,512]{3,2,1,0:T(2,128)(2,1)S(1)} %get-tuple-element.39), channel_id=1, source_target_pairs={{0,1},{1,0},{2,3},{3,2},{4,5},{5,4},{6,7},{7,6},{8,9},{9,8},{10,11... | collective-permute-start | bytes 76808 | tf_op jit(solution)/shard_map/ppermute | solution.py:104
  18.7 1.0 bitcast_convert_fusion
  19.7 1.6 %collective-permute-start.17 = (bf16[1,10,1,1,128]{4,3,1,2,0:T(2,128)(2,1)S(1)}, bf16[1,10,1,1,128]{4,3,1,2,0:T(2,128)(2,1)S(1)}, u32[]{:S(2)}, u32[]{:S(2)}) collective-permute-start(bf16[1,10,1,1,128]{4,3,1,2,0:T(2,128)(2,1)S(1)} %get-tuple-element.78), channel_id=1, source_target_pairs={{0,16},{16,0},{1,17},{17,1},{2,18},{18,2},{3,19},{19,3},{4,20},{20... | collective-permute-start | bytes 7688 | tf_op jit(solution)/shard_map/ppermute | solution.py:20
  22.1 1.3 collective-permute-done.17
  23.4 2.4 %collective-permute-start.1 = (bf16[1,25,1,512]{3,2,1,0:T(2,128)(2,1)S(1)}, bf16[1,25,1,512]{3,2,1,0:T(2,128)(2,1)S(1)}, u32[]{:S(2)}, u32[]{:S(2)}) collective-permute-start(bf16[1,25,1,512]{3,2,1,0:T(2,128)(2,1)S(1)} %get-tuple-element.38), channel_id=1, source_target_pairs={{0,2},{1,3},{2,0},{3,1},{4,6},{5,7},{6,4},{7,5},{8,10},{9,11},{10,... | collective-permute-start | bytes 76808 | tf_op jit(solution)/shard_map/ppermute | solution.py:104
  25.8 1.6 %collective-permute-start.3 = (bf16[1,25,1,512]{3,2,1,0:T(2,128)(2,1)S(1)}, bf16[1,25,1,512]{3,2,1,0:T(2,128)(2,1)S(1)}, u32[]{:S(2)}, u32[]{:S(2)}) collective-permute-start(bf16[1,25,1,512]{3,2,1,0:T(2,128)(2,1)S(1)} %get-tuple-element.36), channel_id=1, source_target_pairs={{0,4},{1,5},{2,6},{3,7},{4,0},{5,1},{6,2},{7,3},{8,12},{9,13},{10,... | collective-permute-start | bytes 76808 | tf_op jit(solution)/shard_map/ppermute | solution.py:104
  27.8 1.1 collective-permute-start.4
  28.9 0.8 collective-permute-done.2
  29.8 2.2 %collective-permute-start.5 = (bf16[1,25,1,512]{3,2,1,0:T(2,128)(2,1)S(1)}, bf16[1,25,1,512]{3,2,1,0:T(2,128)(2,1)S(1)}, u32[]{:S(2)}, u32[]{:S(2)}) collective-permute-start(bf16[1,25,1,512]{3,2,1,0:T(2,128)(2,1)S(1)} %get-tuple-element.34), channel_id=1, source_target_pairs={{0,6},{1,7},{2,4},{3,5},{4,2},{5,3},{6,0},{7,1},{8,14},{9,15},{10,... | collective-permute-start | bytes 76808 | tf_op jit(solution)/shard_map/ppermute | solution.py:104
  32.3 2.7 %collective-permute-start.7 = (bf16[1,25,1,512]{3,2,1,0:T(2,128)(2,1)S(1)}, bf16[1,25,1,512]{3,2,1,0:T(2,128)(2,1)S(1)}, u32[]{:S(2)}, u32[]{:S(2)}) collective-permute-start(bf16[1,25,1,512]{3,2,1,0:T(2,128)(2,1)S(1)} %get-tuple-element.32), channel_id=1, source_target_pairs={{0,8},{1,9},{2,10},{3,11},{4,12},{5,13},{6,14},{7,15},{8,0},{9,1},... | collective-permute-start | bytes 76808 | tf_op jit(solution)/shard_map/ppermute | solution.py:104
  35.0 1.0 collective-permute-start.8
  36.0 0.7 collective-permute-done.6
  36.7 2.1 %collective-permute-start.9 = (bf16[1,25,1,512]{3,2,1,0:T(2,128)(2,1)S(1)}, bf16[1,25,1,512]{3,2,1,0:T(2,128)(2,1)S(1)}, u32[]{:S(2)}, u32[]{:S(2)}) collective-permute-start(bf16[1,25,1,512]{3,2,1,0:T(2,128)(2,1)S(1)} %get-tuple-element.30), channel_id=1, source_target_pairs={{0,10},{1,11},{2,8},{3,9},{4,14},{5,15},{6,12},{7,13},{8,2},{9,3},... | collective-permute-start | bytes 76808 | tf_op jit(solution)/shard_map/ppermute | solution.py:104
  38.8 2.4 %collective-permute-start.10 = (bf16[1,25,1,512]{3,2,1,0:T(2,128)(2,1)S(1)}, bf16[1,25,1,512]{3,2,1,0:T(2,128)(2,1)S(1)}, u32[]{:S(2)}, u32[]{:S(2)}) collective-permute-start(bf16[1,25,1,512]{3,2,1,0:T(2,128)(2,1)S(1)} %get-tuple-element.29), channel_id=1, source_target_pairs={{0,11},{1,10},{2,9},{3,8},{4,15},{5,14},{6,13},{7,12},{8,3},{9,2},... | collective-permute-start | bytes 76808 | tf_op jit(solution)/shard_map/ppermute | solution.py:104
  41.2 2.1 %collective-permute-start.11 = (bf16[1,25,1,512]{3,2,1,0:T(2,128)(2,1)S(1)}, bf16[1,25,1,512]{3,2,1,0:T(2,128)(2,1)S(1)}, u32[]{:S(2)}, u32[]{:S(2)}) collective-permute-start(bf16[1,25,1,512]{3,2,1,0:T(2,128)(2,1)S(1)} %get-tuple-element.28), channel_id=1, source_target_pairs={{0,12},{1,13},{2,14},{3,15},{4,8},{5,9},{6,10},{7,11},{8,4},{9,5},... | collective-permute-start | bytes 76808 | tf_op jit(solution)/shard_map/ppermute | solution.py:104
  43.3 0.7 collective-permute-done.9
  44.0 2.5 %collective-permute-start.12 = (bf16[1,25,1,512]{3,2,1,0:T(2,128)(2,1)S(1)}, bf16[1,25,1,512]{3,2,1,0:T(2,128)(2,1)S(1)}, u32[]{:S(2)}, u32[]{:S(2)}) collective-permute-start(bf16[1,25,1,512]{3,2,1,0:T(2,128)(2,1)S(1)} %get-tuple-element.27), channel_id=1, source_target_pairs={{0,13},{1,12},{2,15},{3,14},{4,9},{5,8},{6,11},{7,10},{8,5},{9,4},... | collective-permute-start | bytes 76808 | tf_op jit(solution)/shard_map/ppermute | solution.py:104
  46.4 3.7 %collective-permute-start.13 = (bf16[1,25,1,512]{3,2,1,0:T(2,128)(2,1)S(1)}, bf16[1,25,1,512]{3,2,1,0:T(2,128)(2,1)S(1)}, u32[]{:S(2)}, u32[]{:S(2)}) collective-permute-start(bf16[1,25,1,512]{3,2,1,0:T(2,128)(2,1)S(1)} %get-tuple-element.41), channel_id=1, source_target_pairs={{0,14},{1,15},{2,12},{3,13},{4,10},{5,11},{6,8},{7,9},{8,6},{9,7},... | collective-permute-start | bytes 76808 | tf_op jit(solution)/shard_map/ppermute | solution.py:104
  50.2 2.0 %collective-permute-start.14 = (bf16[1,25,1,512]{3,2,1,0:T(2,128)(2,1)S(1)}, bf16[1,25,1,512]{3,2,1,0:T(2,128)(2,1)S(1)}, u32[]{:S(2)}, u32[]{:S(2)}) collective-permute-start(bf16[1,25,1,512]{3,2,1,0:T(2,128)(2,1)S(1)} %get-tuple-element.26), channel_id=1, source_target_pairs={{0,15},{1,14},{2,13},{3,12},{4,11},{5,10},{6,9},{7,8},{8,7},{9,6},... | collective-permute-start | bytes 76808 | tf_op jit(solution)/shard_map/ppermute | solution.py:104
  52.2 1.2 collective-permute-done.13
  53.4 3.2 %collective-permute-done.14 = bf16[1,25,1,512]{3,2,1,0:T(2,128)(2,1)S(1)} collective-permute-done((bf16[1,25,1,512]{3,2,1,0:T(2,128)(2,1)S(1)}, bf16[1,25,1,512]{3,2,1,0:T(2,128)(2,1)S(1)}, u32[]{:S(2)}, u32[]{:S(2)}) %collective-permute-start.14) | collective-permute-done | bytes 25632 | tf_op jit(solution)/shard_map/ppermute | solution.py:104
  58.1 1.3 collective-permute-start.19
  59.4 3.1 %collective-permute-start.20 = (f32[1,10,1,64,128]{4,3,1,2,0:T(8,128)S(1)}, f32[1,10,1,64,128]{4,3,1,2,0:T(8,128)S(1)}, u32[]{:S(2)}, u32[]{:S(2)}) collective-permute-start(f32[1,10,1,64,128]{4,3,1,2,0:T(8,128)S(1)} %get-tuple-element.19), channel_id=1, source_target_pairs={{0,1},{1,2},{2,3},{3,4},{4,5},{5,6},{6,7},{7,8},{8,9},{9,10},{10,1... | collective-permute-start | bytes 983048 | tf_op jit(solution)/shard_map/ppermute | solution.py:20
  62.4 1.5 %collective-permute-start.21 = (bf16[1,10,1,1,128]{4,3,1,2,0:T(2,128)(2,1)S(1)}, bf16[1,10,1,1,128]{4,3,1,2,0:T(2,128)(2,1)S(1)}, u32[]{:S(2)}, u32[]{:S(2)}) collective-permute-start(bf16[1,10,1,1,128]{4,3,1,2,0:T(2,128)(2,1)S(1)} %get-tuple-element.76), channel_id=1, source_target_pairs={{0,16},{16,0},{1,17},{17,1},{2,18},{18,2},{3,19},{19,3},{4,20},{20... | collective-permute-start | bytes 7688 | tf_op jit(solution)/shard_map/ppermute | solution.py:20
  64.6 1.6 %collective-permute-done.21 = bf16[1,10,1,1,128]{4,3,1,2,0:T(2,128)(2,1)S(1)} collective-permute-done((bf16[1,10,1,1,128]{4,3,1,2,0:T(2,128)(2,1)S(1)}, bf16[1,10,1,1,128]{4,3,1,2,0:T(2,128)(2,1)S(1)}, u32[]{:S(2)}, u32[]{:S(2)}) %collective-permute-start.21) | collective-permute-done | bytes 2592 | tf_op jit(solution)/shard_map/ppermute | solution.py:20
  66.1 1.4 %collective-permute-done.22 = bf16[1,10,1,1,128]{4,3,1,2,0:T(2,128)(2,1)S(1)} collective-permute-done((bf16[1,10,1,1,128]{4,3,1,2,0:T(2,128)(2,1)S(1)}, bf16[1,10,1,1,128]{4,3,1,2,0:T(2,128)(2,1)S(1)}, u32[]{:S(2)}, u32[]{:S(2)}) %collective-permute-start.22) | collective-permute-done | bytes 2592 | tf_op jit(solution)/shard_map/ppermute | solution.py:21
  68.6 2.3 %scatter_custom_fusion = f32[6,4096]{0,1:T(8,128)} fusion(s32[64]{0:T(128)S(1)} %fusion.49, f32[]{:T(128)} %constant.64.clone.1, f32[6,1,64]{0,2,1:T(8,128)S(1)} %copy.115), kind=kCustom, calls=%fused_computation.1 | custom fusion | flops 384 | bytes 131076 | tf_op jit(solution)/shard_map/scatter-add | solution.py:134
  70.9 61.9 %reduce-scatter.2.cloned.1.call-done = f32[6,256]{0,1:T(8,128)} async-done(((f32[6,4096]{0,1:T(8,128)}), f32[6,256]{0,1:T(8,128)}) %reduce-scatter.2.cloned.1.call-update) | async-done | bytes 6160 | tf_op jit(solution)/shard_map/reduce_scatter | solution.py:135
  132.7 1.6 %copy.113 = f32[1,6,256]{2,0,1:T(1,128)} copy(f32[1,6,256]{1,2,0:T(8,128)} %bitcast.90) | data formatting | bytes 12288
  (85 shorter events, 4.4 us)
Async XLA Ops:
  7.2 14.6 %copy-start = (f32[1,10,1,64,128]{4,3,2,1,0:T(8,128)S(1)}, f32[1,10,1,64,128]{4,3,2,1,0:T(8,128)}, u32[]{:S(2)}) copy-start(f32[1,10,1,64,128]{4,3,2,1,0:T(8,128)} %param.10) | copy-start | bytes 983044
  7.2 14.6 %copy-start.3 = (f32[1,1,64,128]{3,2,1,0:T(8,128)S(1)}, f32[1,1,64,128]{3,2,1,0:T(8,128)}, u32[]{:S(2)}) copy-start(f32[1,1,64,128]{3,2,1,0:T(8,128)} %param.14) | copy-start | bytes 98308
  7.2 14.7 %copy-start.8 = (s32[1,64,1]{1,2,0:T(1,128)S(1)}, s32[1,64,1]{1,2,0:T(1,128)}, u32[]{:S(2)}) copy-start(s32[1,64,1]{1,2,0:T(1,128)} %param.16) | copy-start | bytes 772
  7.2 14.7 %copy-start.7 = (s32[1,64]{1,0:T(1,128)S(1)}, s32[1,64]{1,0:T(1,128)}, u32[]{:S(2)}) copy-start(s32[1,64]{1,0:T(1,128)} %param.17) | copy-start | bytes 772
  7.2 125.5 %reduce-scatter.2.cloned.1.call-start = ((), (), s32[]{:S(2)}) async-start(), calls=%async_computation.1 | async-start | bytes 2228224 | tf_op jit(solution)/shard_map/reduce_scatter | solution.py:135
  7.3 49.6 %collective-permute-start.15 = (f32[1,10,1,64,128]{4,3,1,2,0:T(8,128)}, f32[1,10,1,64,128]{4,3,1,2,0:T(8,128)S(1)}, u32[]{:S(2)}, u32[]{:S(2)}) collective-permute-start(f32[1,10,1,64,128]{4,3,1,2,0:T(8,128)} %bitcast.77), channel_id=1, source_target_pairs={{1,0},{2,1},{3,2},{4,3},{5,4},{6,5},{7,6},{8,7},{9,8},{10,9},{11,1... | collective-permute-start | bytes 983048 | tf_op jit(solution)/shard_map/ppermute | solution.py:21
  8.7 48.2 %collective-permute-start.16 = (f32[1,10,1,64,128]{4,3,1,2,0:T(8,128)}, f32[1,10,1,64,128]{4,3,1,2,0:T(8,128)S(1)}, u32[]{:S(2)}, u32[]{:S(2)}) collective-permute-start(f32[1,10,1,64,128]{4,3,1,2,0:T(8,128)} %bitcast.78), channel_id=1, source_target_pairs={{0,1},{1,2},{2,3},{3,4},{4,5},{5,6},{6,7},{7,8},{8,9},{9,10},{10,1... | collective-permute-start | bytes 983048 | tf_op jit(solution)/shard_map/ppermute | solution.py:20
  16.0 9.8 %collective-permute-start = (bf16[1,25,1,512]{3,2,1,0:T(2,128)(2,1)S(1)}, bf16[1,25,1,512]{3,2,1,0:T(2,128)(2,1)S(1)}, u32[]{:S(2)}, u32[]{:S(2)}) collective-permute-start(bf16[1,25,1,512]{3,2,1,0:T(2,128)(2,1)S(1)} %get-tuple-element.39), channel_id=1, source_target_pairs={{0,1},{1,0},{2,3},{3,2},{4,5},{5,4},{6,7},{7,6},{8,9},{9,8},{10,11... | collective-permute-start | bytes 76808 | tf_op jit(solution)/shard_map/ppermute | solution.py:104
  19.7 3.7 %collective-permute-start.17 = (bf16[1,10,1,1,128]{4,3,1,2,0:T(2,128)(2,1)S(1)}, bf16[1,10,1,1,128]{4,3,1,2,0:T(2,128)(2,1)S(1)}, u32[]{:S(2)}, u32[]{:S(2)}) collective-permute-start(bf16[1,10,1,1,128]{4,3,1,2,0:T(2,128)(2,1)S(1)} %get-tuple-element.78), channel_id=1, source_target_pairs={{0,16},{16,0},{1,17},{17,1},{2,18},{18,2},{3,19},{19,3},{4,20},{20... | collective-permute-start | bytes 7688 | tf_op jit(solution)/shard_map/ppermute | solution.py:20
  21.3 4.5 %collective-permute-start.18 = (bf16[1,10,1,1,128]{4,3,1,2,0:T(2,128)(2,1)S(1)}, bf16[1,10,1,1,128]{4,3,1,2,0:T(2,128)(2,1)S(1)}, u32[]{:S(2)}, u32[]{:S(2)}) collective-permute-start(bf16[1,10,1,1,128]{4,3,1,2,0:T(2,128)(2,1)S(1)} %get-tuple-element.79), channel_id=1, source_target_pairs={{16,0},{0,16},{17,1},{1,17},{18,2},{2,18},{19,3},{3,19},{20,4},{4,... | collective-permute-start | bytes 7688 | tf_op jit(solution)/shard_map/ppermute | solution.py:21
  23.4 4.4 %collective-permute-start.1 = (bf16[1,25,1,512]{3,2,1,0:T(2,128)(2,1)S(1)}, bf16[1,25,1,512]{3,2,1,0:T(2,128)(2,1)S(1)}, u32[]{:S(2)}, u32[]{:S(2)}) collective-permute-start(bf16[1,25,1,512]{3,2,1,0:T(2,128)(2,1)S(1)} %get-tuple-element.38), channel_id=1, source_target_pairs={{0,2},{1,3},{2,0},{3,1},{4,6},{5,7},{6,4},{7,5},{8,10},{9,11},{10,... | collective-permute-start | bytes 76808 | tf_op jit(solution)/shard_map/ppermute | solution.py:104
  25.7 4.0 %collective-permute-start.2 = (bf16[1,25,1,512]{3,2,1,0:T(2,128)(2,1)S(1)}, bf16[1,25,1,512]{3,2,1,0:T(2,128)(2,1)S(1)}, u32[]{:S(2)}, u32[]{:S(2)}) collective-permute-start(bf16[1,25,1,512]{3,2,1,0:T(2,128)(2,1)S(1)} %get-tuple-element.37), channel_id=1, source_target_pairs={{0,3},{1,2},{2,1},{3,0},{4,7},{5,6},{6,5},{7,4},{8,11},{9,10},{10,... | collective-permute-start | bytes 76808 | tf_op jit(solution)/shard_map/ppermute | solution.py:104
  25.8 6.1 %collective-permute-start.3 = (bf16[1,25,1,512]{3,2,1,0:T(2,128)(2,1)S(1)}, bf16[1,25,1,512]{3,2,1,0:T(2,128)(2,1)S(1)}, u32[]{:S(2)}, u32[]{:S(2)}) collective-permute-start(bf16[1,25,1,512]{3,2,1,0:T(2,128)(2,1)S(1)} %get-tuple-element.36), channel_id=1, source_target_pairs={{0,4},{1,5},{2,6},{3,7},{4,0},{5,1},{6,2},{7,3},{8,12},{9,13},{10,... | collective-permute-start | bytes 76808 | tf_op jit(solution)/shard_map/ppermute | solution.py:104
  27.8 4.5 %collective-permute-start.4 = (bf16[1,25,1,512]{3,2,1,0:T(2,128)(2,1)S(1)}, bf16[1,25,1,512]{3,2,1,0:T(2,128)(2,1)S(1)}, u32[]{:S(2)}, u32[]{:S(2)}) collective-permute-start(bf16[1,25,1,512]{3,2,1,0:T(2,128)(2,1)S(1)} %get-tuple-element.35), channel_id=1, source_target_pairs={{0,5},{1,4},{2,7},{3,6},{4,1},{5,0},{6,3},{7,2},{8,13},{9,12},{10,... | collective-permute-start | bytes 76808 | tf_op jit(solution)/shard_map/ppermute | solution.py:104
  29.8 5.2 %collective-permute-start.5 = (bf16[1,25,1,512]{3,2,1,0:T(2,128)(2,1)S(1)}, bf16[1,25,1,512]{3,2,1,0:T(2,128)(2,1)S(1)}, u32[]{:S(2)}, u32[]{:S(2)}) collective-permute-start(bf16[1,25,1,512]{3,2,1,0:T(2,128)(2,1)S(1)} %get-tuple-element.34), channel_id=1, source_target_pairs={{0,6},{1,7},{2,4},{3,5},{4,2},{5,3},{6,0},{7,1},{8,14},{9,15},{10,... | collective-permute-start | bytes 76808 | tf_op jit(solution)/shard_map/ppermute | solution.py:104
  32.0 4.7 %collective-permute-start.6 = (bf16[1,25,1,512]{3,2,1,0:T(2,128)(2,1)S(1)}, bf16[1,25,1,512]{3,2,1,0:T(2,128)(2,1)S(1)}, u32[]{:S(2)}, u32[]{:S(2)}) collective-permute-start(bf16[1,25,1,512]{3,2,1,0:T(2,128)(2,1)S(1)} %get-tuple-element.33), channel_id=1, source_target_pairs={{0,7},{1,6},{2,5},{3,4},{4,3},{5,2},{6,1},{7,0},{8,15},{9,14},{10,... | collective-permute-start | bytes 76808 | tf_op jit(solution)/shard_map/ppermute | solution.py:104
  32.3 6.4 %collective-permute-start.7 = (bf16[1,25,1,512]{3,2,1,0:T(2,128)(2,1)S(1)}, bf16[1,25,1,512]{3,2,1,0:T(2,128)(2,1)S(1)}, u32[]{:S(2)}, u32[]{:S(2)}) collective-permute-start(bf16[1,25,1,512]{3,2,1,0:T(2,128)(2,1)S(1)} %get-tuple-element.32), channel_id=1, source_target_pairs={{0,8},{1,9},{2,10},{3,11},{4,12},{5,13},{6,14},{7,15},{8,0},{9,1},... | collective-permute-start | bytes 76808 | tf_op jit(solution)/shard_map/ppermute | solution.py:104
  35.0 6.2 %collective-permute-start.8 = (bf16[1,25,1,512]{3,2,1,0:T(2,128)(2,1)S(1)}, bf16[1,25,1,512]{3,2,1,0:T(2,128)(2,1)S(1)}, u32[]{:S(2)}, u32[]{:S(2)}) collective-permute-start(bf16[1,25,1,512]{3,2,1,0:T(2,128)(2,1)S(1)} %get-tuple-element.31), channel_id=1, source_target_pairs={{0,9},{1,8},{2,11},{3,10},{4,13},{5,12},{6,15},{7,14},{8,1},{9,0},... | collective-permute-start | bytes 76808 | tf_op jit(solution)/shard_map/ppermute | solution.py:104
  36.7 7.3 %collective-permute-start.9 = (bf16[1,25,1,512]{3,2,1,0:T(2,128)(2,1)S(1)}, bf16[1,25,1,512]{3,2,1,0:T(2,128)(2,1)S(1)}, u32[]{:S(2)}, u32[]{:S(2)}) collective-permute-start(bf16[1,25,1,512]{3,2,1,0:T(2,128)(2,1)S(1)} %get-tuple-element.30), channel_id=1, source_target_pairs={{0,10},{1,11},{2,8},{3,9},{4,14},{5,15},{6,12},{7,13},{8,2},{9,3},... | collective-permute-start | bytes 76808 | tf_op jit(solution)/shard_map/ppermute | solution.py:104
  38.8 7.7 %collective-permute-start.10 = (bf16[1,25,1,512]{3,2,1,0:T(2,128)(2,1)S(1)}, bf16[1,25,1,512]{3,2,1,0:T(2,128)(2,1)S(1)}, u32[]{:S(2)}, u32[]{:S(2)}) collective-permute-start(bf16[1,25,1,512]{3,2,1,0:T(2,128)(2,1)S(1)} %get-tuple-element.29), channel_id=1, source_target_pairs={{0,11},{1,10},{2,9},{3,8},{4,15},{5,14},{6,13},{7,12},{8,3},{9,2},... | collective-permute-start | bytes 76808 | tf_op jit(solution)/shard_map/ppermute | solution.py:104
  41.2 9.0 %collective-permute-start.11 = (bf16[1,25,1,512]{3,2,1,0:T(2,128)(2,1)S(1)}, bf16[1,25,1,512]{3,2,1,0:T(2,128)(2,1)S(1)}, u32[]{:S(2)}, u32[]{:S(2)}) collective-permute-start(bf16[1,25,1,512]{3,2,1,0:T(2,128)(2,1)S(1)} %get-tuple-element.28), channel_id=1, source_target_pairs={{0,12},{1,13},{2,14},{3,15},{4,8},{5,9},{6,10},{7,11},{8,4},{9,5},... | collective-permute-start | bytes 76808 | tf_op jit(solution)/shard_map/ppermute | solution.py:104
  44.0 8.2 %collective-permute-start.12 = (bf16[1,25,1,512]{3,2,1,0:T(2,128)(2,1)S(1)}, bf16[1,25,1,512]{3,2,1,0:T(2,128)(2,1)S(1)}, u32[]{:S(2)}, u32[]{:S(2)}) collective-permute-start(bf16[1,25,1,512]{3,2,1,0:T(2,128)(2,1)S(1)} %get-tuple-element.27), channel_id=1, source_target_pairs={{0,13},{1,12},{2,15},{3,14},{4,9},{5,8},{6,11},{7,10},{8,5},{9,4},... | collective-permute-start | bytes 76808 | tf_op jit(solution)/shard_map/ppermute | solution.py:104
  46.4 7.0 %collective-permute-start.13 = (bf16[1,25,1,512]{3,2,1,0:T(2,128)(2,1)S(1)}, bf16[1,25,1,512]{3,2,1,0:T(2,128)(2,1)S(1)}, u32[]{:S(2)}, u32[]{:S(2)}) collective-permute-start(bf16[1,25,1,512]{3,2,1,0:T(2,128)(2,1)S(1)} %get-tuple-element.41), channel_id=1, source_target_pairs={{0,14},{1,15},{2,12},{3,13},{4,10},{5,11},{6,8},{7,9},{8,6},{9,7},... | collective-permute-start | bytes 76808 | tf_op jit(solution)/shard_map/ppermute | solution.py:104
  50.2 6.4 %collective-permute-start.14 = (bf16[1,25,1,512]{3,2,1,0:T(2,128)(2,1)S(1)}, bf16[1,25,1,512]{3,2,1,0:T(2,128)(2,1)S(1)}, u32[]{:S(2)}, u32[]{:S(2)}) collective-permute-start(bf16[1,25,1,512]{3,2,1,0:T(2,128)(2,1)S(1)} %get-tuple-element.26), channel_id=1, source_target_pairs={{0,15},{1,14},{2,13},{3,12},{4,11},{5,10},{6,9},{7,8},{8,7},{9,6},... | collective-permute-start | bytes 76808 | tf_op jit(solution)/shard_map/ppermute | solution.py:104
  56.8 1.0 copy-start.1
  56.8 1.0 copy-start.4
  56.8 1.0 copy-start.5
  58.1 9.6 %collective-permute-start.19 = (f32[1,10,1,64,128]{4,3,1,2,0:T(8,128)S(1)}, f32[1,10,1,64,128]{4,3,1,2,0:T(8,128)S(1)}, u32[]{:S(2)}, u32[]{:S(2)}) collective-permute-start(f32[1,10,1,64,128]{4,3,1,2,0:T(8,128)S(1)} %get-tuple-element.19), channel_id=1, source_target_pairs={{1,0},{2,1},{3,2},{4,3},{5,4},{6,5},{7,6},{8,7},{9,8},{10,9},{11,1... | collective-permute-start | bytes 983048 | tf_op jit(solution)/shard_map/ppermute | solution.py:21
  59.4 8.3 %collective-permute-start.20 = (f32[1,10,1,64,128]{4,3,1,2,0:T(8,128)S(1)}, f32[1,10,1,64,128]{4,3,1,2,0:T(8,128)S(1)}, u32[]{:S(2)}, u32[]{:S(2)}) collective-permute-start(f32[1,10,1,64,128]{4,3,1,2,0:T(8,128)S(1)} %get-tuple-element.19), channel_id=1, source_target_pairs={{0,1},{1,2},{2,3},{3,4},{4,5},{5,6},{6,7},{7,8},{8,9},{9,10},{10,1... | collective-permute-start | bytes 983048 | tf_op jit(solution)/shard_map/ppermute | solution.py:20
  62.4 3.7 %collective-permute-start.21 = (bf16[1,10,1,1,128]{4,3,1,2,0:T(2,128)(2,1)S(1)}, bf16[1,10,1,1,128]{4,3,1,2,0:T(2,128)(2,1)S(1)}, u32[]{:S(2)}, u32[]{:S(2)}) collective-permute-start(bf16[1,10,1,1,128]{4,3,1,2,0:T(2,128)(2,1)S(1)} %get-tuple-element.76), channel_id=1, source_target_pairs={{0,16},{16,0},{1,17},{17,1},{2,18},{18,2},{3,19},{19,3},{4,20},{20... | collective-permute-start | bytes 7688 | tf_op jit(solution)/shard_map/ppermute | solution.py:20
  63.9 3.6 %collective-permute-start.22 = (bf16[1,10,1,1,128]{4,3,1,2,0:T(2,128)(2,1)S(1)}, bf16[1,10,1,1,128]{4,3,1,2,0:T(2,128)(2,1)S(1)}, u32[]{:S(2)}, u32[]{:S(2)}) collective-permute-start(bf16[1,10,1,1,128]{4,3,1,2,0:T(2,128)(2,1)S(1)} %get-tuple-element.77), channel_id=1, source_target_pairs={{16,0},{0,16},{17,1},{1,17},{18,2},{2,18},{19,3},{3,19},{20,4},{4,... | collective-permute-start | bytes 7688 | tf_op jit(solution)/shard_map/ppermute | solution.py:21
  68.3 2.6 %copy-start.2 = (f32[1,10,1,64,128]{4,3,1,2,0:T(8,128)}, f32[1,10,1,64,128]{4,3,1,2,0:T(8,128)S(1)}, u32[]{:S(2)}) copy-start(f32[1,10,1,64,128]{4,3,1,2,0:T(8,128)S(1)} %fusion.17) | copy-start | bytes 983044
  (1 other events, 0.7 us)
Sparse Core Ops, SparseCore 0:
  71.0 61.7 reduce-scatter.1
